TPU v7x, 128 devices: a whole 4x4x4 slice. The times are simulated.
128 devices in a mesh: rows: 32 (over x, z, core), units: 4 (over y).
Axes of the slice: x: 4, y: 4, z: 4, core: 2. Of those that a mesh axis runs over, the one named last changes fastest.
Arguments:
- residuals: bfloat16 [524288, 2048], P(('rows', 'units')), may hold values from -24 to 24
- loadings: bfloat16 [524288, 256], P(('rows', 'units')), may hold values from -6 to 6
- zero_points: bfloat16 [1024, 2048], P('units'), may hold values from -0.375 to 0.375
- sketch_matrix: bfloat16 [2048, 256], replicated, may hold values from -0.125 to 0.125
- use_lists: int32 [4096, 4], P(('rows', 'units')), may hold values from 0 to 15, all different within a row
Outputs:
- star_basis: float32 [524288, 256], P(('rows', 'units'))
- bin_modes: float32 [2048, 256], P(('rows', 'units'))
Inputs may be any that keep to these rules, and one draw needn't show every extreme that they name: `use_lists`: each row names 4 different groups; every group is named by some row.
All inputs are finite; a program needn't handle non-finite values.
Results may differ from a plain program's by a relative error of at most 0.003.
Values may be sent and summed in bfloat16 or wider, within the bound.
No kernel may reach another device: no remote copies, remote signals or barrier semaphores. Data moves between devices by JAX's collectives and lax.ppermute only.
A program may use at most 192 MiB of HBM per device.

v0:
```python
import jax
import jax.numpy as jnp
from jax import lax
from jax.sharding import PartitionSpec as P

GROUP = 64
USES = 4
BLOCK_STARS = 128


def on_device(residuals, loadings, zero_points, sketch_matrix, use_lists):
    gathered = lax.all_gather(zero_points, "units", axis=0, tiled=True)
    local_rows, width_bins = residuals.shape
    group_count = gathered.shape[0] // GROUP
    block_count = use_lists.shape[0]
    tables = gathered.reshape(group_count, GROUP, width_bins)
    chosen = tables[use_lists].reshape(block_count, USES * GROUP, width_bins)
    offsets = jnp.einsum(
        "bsk,bkn->bsn",
        loadings.reshape(block_count, BLOCK_STARS, USES * GROUP),
        chosen,
        preferred_element_type=jnp.float32,
    )
    corrected = (
        residuals.reshape(block_count, BLOCK_STARS, width_bins).astype(jnp.float32) - offsets
    ).astype(jnp.bfloat16)
    corrected = corrected.reshape(local_rows, width_bins)
    sketched = jnp.dot(corrected, sketch_matrix, preferred_element_type=jnp.float32)
    sketch_low = sketched.astype(jnp.bfloat16)
    devices_all = lax.axis_size(("rows", "units"))
    total_stars = local_rows * devices_all
    gram_local = jnp.dot(sketched.T, sketched, precision=lax.Precision.HIGHEST) / total_stars
    lower_factor = jnp.linalg.cholesky(lax.psum(gram_local, ("rows", "units")))
    star_basis = lax.linalg.triangular_solve(
        lower_factor, sketched, left_side=False, lower=True, transpose_a=True
    )
    bin_share = width_bins // devices_all
    full_terms = jnp.einsum("sn,sm->nm", corrected, sketch_low, preferred_element_type=jnp.float32)
    summed_all = lax.psum(full_terms, ("rows", "units"))
    first_bin = lax.axis_index(("rows", "units")) * bin_share
    summed = lax.dynamic_slice_in_dim(summed_all, first_bin, bin_share, 0)
    raw_modes = summed / total_stars
    bin_modes = lax.linalg.triangular_solve(
        lower_factor, raw_modes, left_side=False, lower=True, transpose_a=True
    )
    return (star_basis, bin_modes)


def solution(mesh):
    in_specs = (
        P(("rows", "units"), None),
        P(("rows", "units"), None),
        P("units", None),
        P(),
        P(("rows", "units"), None),
    )
    out_specs = (P(("rows", "units"), None), P(("rows", "units"), None))
    return jax.shard_map(
        on_device, mesh=mesh, in_specs=in_specs, out_specs=out_specs, check_vma=False
    )
```

profile of v0, /device:TPU:1, one launch (start us, length us, event | category | flops | bytes accessed | tf_op | source)
XLA Modules:
  0.0 364.4 jit_solution(14588423251606039512)
XLA Ops:
  8.0 0.7 compare_select_fusion
  8.9 52.1 %all-gather.2.cloned.1.call-done = bf16[1024,2048]{1,0:T(8,128)(2,1)} async-done(((bf16[256,2048]{1,0:T(8,128)(2,1)}), bf16[1024,2048]{1,0:T(8,128)(2,1)}) %all-gather.2.cloned.1.call-update) | async-done | bytes 4194320 | tf_op jit(solution)/shard_map/all_gather | solution.py:12
  60.9 14.9 %gather_fusion = bf16[128,64,2048]{2,1,0:T(8,128)(2,1)} fusion(bf16[16,64,2048]{2,1,0:T(8,128)(2,1)} %bitcast.51, s32[1024]{0:T(1024)S(1)} %pad_clamp_fusion), kind=kCustom, calls=%fused_computation | custom fusion | bytes 67109376 | tf_op jit(solution)/shard_map/gather | solution.py:17
  75.8 23.4 %fusion = bf16[32,128,2048]{2,1,0:T(8,128)(2,1)} fusion(bf16[32,128,2048]{2,1,0:T(8,128)(2,1)} %bitcast.53, bf16[32,128,256]{2,1,0:T(8,128)(2,1)S(1)} %bitcast.50, bf16[32,256,2048]{2,1,0:T(8,128)(2,1)} %bitcast.52), kind=kOutput, calls=%fused_computation.4 | convolution fusion | flops 4320133120 | bytes 69206016 | tf_op jit(solution)/shard_map/bsk,bkn->bsn/dot_general | solution.py:18
  99.3 10.3 %fusion.16 = f32[4096,256]{1,0:T(8,128)S(1)} fusion(bf16[4096,2048]{1,0:T(8,128)(2,1)} %bitcast.54, bf16[2048,256]{1,0:T(8,128)(2,1)S(1)} %copy-done.5), kind=kOutput, calls=%fused_computation.44 | convolution fusion | flops 4294967296 | bytes 22020096 | tf_op jit(solution)/shard_map/dot_general | solution.py:28
  109.8 6.3 %fusion.3 = f32[2048,256]{1,0:T(8,128)} fusion(bf16[4096,2048]{1,0:T(8,128)(2,1)S(1)} %bitcast.55, f32[4096,256]{1,0:T(8,128)S(1)} %fusion.16), kind=kOutput, calls=%fused_computation.9 | convolution fusion | flops 4296015872 | bytes 23068672 | tf_op jit(solution)/shard_map/sn,sm->nm/dot_general | solution.py:38
  116.1 7.4 %convolution_multiply_fusion = f32[256,256]{0,1:T(8,128)} fusion(f32[4096,256]{1,0:T(8,128)S(1)} %fusion.16), kind=kOutput, calls=%fused_computation.11 | convolution fusion | flops 3221291008 | bytes 4456448 | tf_op jit(solution)/shard_map/dot_general | solution.py:32
  123.6 152.5 %all-reduce.4.cloned.1.call-done = (f32[256,256]{0,1:T(8,128)}, f32[2048,256]{1,0:T(8,128)}) async-done(((f32[256,256]{0,1:T(8,128)}, f32[2048,256]{1,0:T(8,128)}), (f32[256,256]{0,1:T(8,128)}, f32[2048,256]{1,0:T(8,128)})) %all-reduce.4.cloned.1.call-update) | async-done | bytes 2359312 | tf_op jit(solution)/shard_map/psum | solution.py:33
  276.1 1.2 copy.13
  277.4 1.0 fusion.5
  278.4 11.7 %cholesky.50 = f32[128,128]{1,0:T(8,128)S(1)} custom-call(f32[128,128]{1,0:T(8,128)S(1)} %cholesky.118), custom_call_target="Cholesky" | custom-call | tf_op jit(solution)/shard_map/jit(cholesky)/cholesky | solution.py:33
  290.1 9.8 %custom-call.16 = f32[1,128,128]{1,2,0:T(8,128)S(1)} custom-call(f32[1,128,128]{2,1,0:T(8,128)S(1)} %get-tuple-element.29), custom_call_target="InvertDiagBlocksLowerTriangular" | custom-call | tf_op jit(solution)/shard_map/jit(cholesky)/cholesky | solution.py:33
  300.5 11.7 %cholesky.105 = f32[128,128]{1,0:T(8,128)S(1)} custom-call(f32[128,128]{1,0:T(8,128)S(1)} %convolution_subtract_fusion.1), custom_call_target="Cholesky" | custom-call | tf_op jit(solution)/shard_map/jit(cholesky)/cholesky | solution.py:33
  312.2 0.7 compare_reduce_fusion
  314.3 3.9 %while.1 = (s32[]{:T(128)}, f32[256,256]{1,0:T(8,128)S(1)}, s32[2,2]{1,0:T(2,128)S(1)}, f32[2,128,128]{2,1,0:T(8,128)S(1)}, s32[]{:T(128)}) while((s32[]{:T(128)}, f32[256,256]{1,0:T(8,128)S(1)}, s32[2,2]{1,0:T(2,128)S(1)}, f32[2,128,128]{2,1,0:T(8,128)S(1)}, s32[]{:T(128)}) %tuple.29), condition=%wide.while_cond, body=%wide.while_body.sunk | while | flops 2 | bytes 131181 | solution.py:34
  314.9 1.3 bitcast_dynamic-update-slice_fusion.2
  316.8 1.3 bitcast_dynamic-update-slice_fusion.2
  318.1 19.9 %custom-call.17 = f32[2,128,128]{1,2,0:T(8,128)S(1)} custom-call(f32[2,128,128]{2,1,0:T(8,128)S(1)} %get-tuple-element.9), custom_call_target="InvertDiagBlocksLowerTriangular" | custom-call | tf_op jit(solution)/shard_map/triangular_solve | solution.py:34
  338.1 3.7 %fusion.1 = f32[4096,128]{0,1:T(8,128)S(1)} fusion(f32[4096,256]{1,0:T(8,128)} %copy-done.2, f32[2,128,128]{1,2,0:T(8,128)S(1)} %custom-call.17), kind=kOutput, calls=%fused_computation.7 | convolution fusion | flops 805306368 | bytes 4259840 | tf_op jit(solution)/shard_map/triangular_solve | solution.py:34
  341.8 0.7 dynamic-slice_multiply_fusion
  343.7 3.6 convolution_subtract_fusion
  347.3 2.0 fusion.11
  349.3 2.4 pad_maximum_fusion
  351.7 5.6 %copy.14 = f32[4096,256]{1,0:T(8,128)} copy(f32[4096,256]{0,1:T(8,128)} %pad_maximum_fusion) | data formatting | bytes 8388608
  (37 shorter events, 4.2 us)
Async XLA Ops:
  7.2 68.7 %copy-start = (bf16[4096,256]{1,0:T(8,128)(2,1)S(1)}, bf16[4096,256]{1,0:T(8,128)(2,1)}, u32[]{:S(2)}) copy-start(bf16[4096,256]{1,0:T(8,128)(2,1)} %param.6) | copy-start | bytes 6291460
  7.2 53.8 %all-gather.2.cloned.1.call-start = ((), (), s32[]{:S(2)}) async-start(), calls=%async_computation | async-start | bytes 5242880 | tf_op jit(solution)/shard_map/all_gather | solution.py:12
  7.9 268.2 %all-reduce.4.cloned.1.call-start = ((), (), s32[]{:S(2)}) async-start(), calls=%async_computation.1 | async-start | bytes 4718592 | tf_op jit(solution)/shard_map/psum | solution.py:33
  75.8 23.4 %copy-start.5 = (bf16[2048,256]{1,0:T(8,128)(2,1)S(1)}, bf16[2048,256]{1,0:T(8,128)(2,1)}, u32[]{:S(2)}) copy-start(bf16[2048,256]{1,0:T(8,128)(2,1)} %param.8) | copy-start | bytes 3145732
  99.3 10.5 %copy-start.4 = (bf16[32,128,2048]{2,1,0:T(8,128)(2,1)S(1)}, bf16[32,128,2048]{2,1,0:T(8,128)(2,1)}, u32[]{:S(2)}) copy-start(bf16[32,128,2048]{2,1,0:T(8,128)(2,1)} %fusion) | copy-start | bytes 50331652
  109.8 6.3 %copy-start.2 = (f32[4096,256]{1,0:T(8,128)}, f32[4096,256]{1,0:T(8,128)S(1)}, u32[]{:S(2)}) copy-start(f32[4096,256]{1,0:T(8,128)S(1)} %fusion.16) | copy-start | bytes 12582916
  338.0 5.7 %copy-start.3 = (f32[4096,256]{1,0:T(8,128)S(1)}, f32[4096,256]{1,0:T(8,128)}, u32[]{:S(2)}) copy-start(f32[4096,256]{1,0:T(8,128)} %copy-done.2) | copy-start | bytes 12582916
  349.3 8.0 %copy-start.1 = (bf16[4096,256]{1,0:T(8,128)(2,1)S(1)}, bf16[4096,256]{1,0:T(8,128)(2,1)}, u32[]{:S(2)}) copy-start(bf16[4096,256]{1,0:T(8,128)(2,1)} %param.6) | copy-start | bytes 6291460
Sparse Core Ops, SparseCore 0:
  9.7 51.2 all-gather.1
  123.7 152.3 all-reduce.3
where the time goes:
time: 369 us; the launch traced here: 364 us
  waiting for transfers between devices  205 us (56%)
  other arithmetic  59.4 us (16%)
  matrix products  57.9 us (16%)
  local copies, waits for them, and re-layouts  26.1 us (7%)
  between operations  15.7 us (4%)
    psum x1, waiting for transfers between devices, on_device(): lower_factor = jnp.linalg.cholesky(lax.psum(gram_local, ('rows', 'units')))  153 us
    all_gather x1, waiting for transfers between devices, on_device(): gathered = lax.all_gather(zero_points, 'units', axis=0, tiled=True)  52.1 us
    another operation x6, other arithmetic, on_device(): lower_factor = jnp.linalg.cholesky(lax.psum(gram_local, ('rows', 'units')))  34 us
    dot_general x1, matrix products, on_device(): jnp.einsum('bsk,bkn->bsn', loadings.reshape(block_count, BLOCK_STARS, USE...  23.4 us
    another operation x4, other arithmetic, on_device(): lax.linalg.triangular_solve(lower_factor, sketched, left_side=False, lowe...  22.3 us
    gather x1, local copies, waits for them, and re-layouts, on_device(): chosen = tables[use_lists].reshape(block_count, USES * GROUP, width_bins)  14.9 us
    dot_general x1, matrix products, on_device(): jnp.dot(corrected, sketch_matrix, preferred_element_type=jnp.float32)  10.3 us
    another operation x3, matrix products, on_device(): lax.linalg.triangular_solve(lower_factor, sketched, left_side=False, lowe...  9.32 us
  transfers between devices with their start and end apart: 2, of which 2 were waited for; matrix products, arithmetic and copies ran while one was open for 0% of the time, Pallas kernels for 0%

commit v1 on v0

--- a/solution.py
+++ b/solution.py
@@ -30,7 +30,9 @@
     devices_all = lax.axis_size(("rows", "units"))
     total_stars = local_rows * devices_all
     gram_local = jnp.dot(sketched.T, sketched, precision=lax.Precision.HIGHEST) / total_stars
-    lower_factor = jnp.linalg.cholesky(lax.psum(gram_local, ("rows", "units")))
+    lower_factor = jnp.linalg.cholesky(
+        jnp.sum(lax.all_gather(gram_local, ("rows", "units")), axis=0)
+    )
     star_basis = lax.linalg.triangular_solve(
         lower_factor, sketched, left_side=False, lower=True, transpose_a=True
     )

time: 369 us -> 482 us (1.31)
  waiting for transfers between devices: 205 us -> 300 us
  other arithmetic: 59.4 us -> 70.5 us
    all_gather x0 -> x1, waiting for transfers between devices: none -> 108 us  [on_device(): lax.all_gather(gram_local, ('rows', 'units'))]
    psum x1, waiting for transfers between devices: 153 us -> 140 us  [on_device(): summed_all = lax.psum(full_terms, ('rows', 'units'))]
    reduce_sum x0 -> x1, other arithmetic: none -> 12.2 us  [on_device(): jnp.sum(lax.all_gather(gram_local, ('rows', 'units')), axis=0)]
  transfers between devices with their start and end apart: 2 -> 3, of which waited for: 2 -> 3; matrix products, arithmetic and copies ran while one was open for 0% -> 3% of each run, Pallas kernels for 0% -> 0%
where the time goes in v1:
time: 482 us; the launch traced here: 475 us
  waiting for transfers between devices  300 us (62%)
  other arithmetic  70.5 us (15%)
  matrix products  61 us (13%)
  local copies, waits for them, and re-layouts  26.8 us (6%)
  between operations  15.4 us (3%)
    psum x1, waiting for transfers between devices, on_device(): summed_all = lax.psum(full_terms, ('rows', 'units'))  140 us
    all_gather x1, waiting for transfers between devices, on_device(): lax.all_gather(gram_local, ('rows', 'units'))  108 us
    all_gather x1, waiting for transfers between devices, on_device(): gathered = lax.all_gather(zero_points, 'units', axis=0, tiled=True)  52.1 us
    another operation x6, other arithmetic, on_device(): jnp.linalg.cholesky(jnp.sum(lax.all_gather(gram_local, ('rows', 'units'))...  34 us
    dot_general x1, matrix products, on_device(): jnp.einsum('bsk,bkn->bsn', loadings.reshape(block_count, BLOCK_STARS, USE...  23.4 us
    another operation x4, other arithmetic, on_device(): lax.linalg.triangular_solve(lower_factor, sketched, left_side=False, lowe...  22.3 us
    gather x1, local copies, waits for them, and re-layouts, on_device(): chosen = tables[use_lists].reshape(block_count, USES * GROUP, width_bins)  14.9 us
    reduce_sum x1, other arithmetic, on_device(): jnp.sum(lax.all_gather(gram_local, ('rows', 'units')), axis=0)  12.2 us
  transfers between devices with their start and end apart: 3, of which 3 were waited for; matrix products, arithmetic and copies ran while one was open for 3% of the time, Pallas kernels for 0%

profile of v1, /device:TPU:1, one launch (start us, length us, event | category | flops | bytes accessed | tf_op | source)
XLA Modules:
  0.0 474.8 jit_solution(12183699995980723788)
XLA Ops:
  8.0 0.7 compare_select_fusion
  8.9 52.1 %all-gather.4.cloned.1.call-done = bf16[1024,2048]{1,0:T(8,128)(2,1)} async-done(((bf16[256,2048]{1,0:T(8,128)(2,1)}), bf16[1024,2048]{1,0:T(8,128)(2,1)}) %all-gather.4.cloned.1.call-update) | async-done | bytes 4194320 | tf_op jit(solution)/shard_map/all_gather | solution.py:12
  60.9 14.9 %gather_fusion = bf16[128,64,2048]{2,1,0:T(8,128)(2,1)} fusion(bf16[16,64,2048]{2,1,0:T(8,128)(2,1)} %bitcast.52, s32[1024]{0:T(1024)S(1)} %pad_clamp_fusion), kind=kCustom, calls=%fused_computation | custom fusion | bytes 67109376 | tf_op jit(solution)/shard_map/gather | solution.py:17
  75.8 23.4 %fusion = bf16[32,128,2048]{2,1,0:T(8,128)(2,1)} fusion(bf16[32,128,2048]{2,1,0:T(8,128)(2,1)} %bitcast.55, bf16[32,128,256]{2,1,0:T(8,128)(2,1)S(1)} %bitcast.51, bf16[32,256,2048]{2,1,0:T(8,128)(2,1)} %bitcast.53), kind=kOutput, calls=%fused_computation.4 | convolution fusion | flops 4320133120 | bytes 69206016 | tf_op jit(solution)/shard_map/bsk,bkn->bsn/dot_general | solution.py:18
  99.3 9.9 %fusion.16 = f32[4096,256]{1,0:T(8,128)S(1)} fusion(bf16[4096,2048]{1,0:T(8,128)(2,1)} %bitcast.56, bf16[2048,256]{1,0:T(8,128)(2,1)S(1)} %copy-done.5), kind=kOutput, calls=%fused_computation.44 | convolution fusion | flops 4294967296 | bytes 22020096 | tf_op jit(solution)/shard_map/dot_general | solution.py:28
  109.2 2.0 copy-done.2
  111.2 6.4 %fusion.3 = f32[2048,256]{1,0:T(8,128)} fusion(bf16[4096,2048]{1,0:T(8,128)(2,1)S(1)} %bitcast.57, f32[4096,256]{1,0:T(8,128)S(1)} %fusion.16), kind=kOutput, calls=%fused_computation.9 | convolution fusion | flops 4296015872 | bytes 23068672 | tf_op jit(solution)/shard_map/sn,sm->nm/dot_general | solution.py:40
  118.1 10.9 %convolution_multiply_fusion = f32[256,256]{1,0:T(8,128)} fusion(f32[4096,256]{1,0:T(8,128)} %copy-done.2), kind=kOutput, calls=%fused_computation.11 | convolution fusion | flops 3221291008 | bytes 4456448 | tf_op jit(solution)/shard_map/dot_general | solution.py:32
  129.1 140.1 %all-reduce.3.cloned.1.call-done = f32[2048,256]{1,0:T(8,128)} async-done(((f32[2048,256]{1,0:T(8,128)}), f32[2048,256]{1,0:T(8,128)}) %all-reduce.3.cloned.1.call-update) | async-done | bytes 2097168 | tf_op jit(solution)/shard_map/psum | solution.py:41
  269.2 0.7 dynamic-slice_multiply_fusion
  269.9 107.6 %all-gather.6.cloned.1.call-done = f32[32768,256]{1,0:T(8,128)} async-done(((f32[256,256]{1,0:T(8,128)}), f32[32768,256]{1,0:T(8,128)}) %all-gather.6.cloned.1.call-update) | async-done | bytes 33554448 | tf_op jit(solution)/shard_map/all_gather | solution.py:34
  377.5 12.2 %reduce_sum.9 = f32[256,256]{1,0:T(8,128)S(1)} reduce(f32[128,256,256]{2,1,0:T(8,128)} %bitcast.54, f32[]{:T(128)} %constant.97.clone.1), dimensions={0}, to_apply=%region_0.0 | reduce | flops 8323072 | bytes 33816580 | tf_op jit(solution)/shard_map/reduce_sum | solution.py:34
  389.8 11.7 %cholesky.50 = f32[128,128]{1,0:T(8,128)S(1)} custom-call(f32[128,128]{1,0:T(8,128)S(1)} %cholesky.118), custom_call_target="Cholesky" | custom-call | tf_op jit(solution)/shard_map/jit(cholesky)/cholesky | solution.py:33
  401.6 9.8 %custom-call.16 = f32[1,128,128]{1,2,0:T(8,128)S(1)} custom-call(f32[1,128,128]{2,1,0:T(8,128)S(1)} %get-tuple-element.29), custom_call_target="InvertDiagBlocksLowerTriangular" | custom-call | tf_op jit(solution)/shard_map/jit(cholesky)/cholesky | solution.py:33
  411.9 11.7 %cholesky.105 = f32[128,128]{1,0:T(8,128)S(1)} custom-call(f32[128,128]{1,0:T(8,128)S(1)} %convolution_subtract_fusion.1), custom_call_target="Cholesky" | custom-call | tf_op jit(solution)/shard_map/jit(cholesky)/cholesky | solution.py:33
  425.7 3.9 while.1
  426.3 1.3 bitcast_dynamic-update-slice_fusion.2
  428.2 1.3 bitcast_dynamic-update-slice_fusion.2
  429.6 19.9 %custom-call.17 = f32[2,128,128]{1,2,0:T(8,128)S(1)} custom-call(f32[2,128,128]{2,1,0:T(8,128)S(1)} %get-tuple-element.9), custom_call_target="InvertDiagBlocksLowerTriangular" | custom-call | tf_op jit(solution)/shard_map/triangular_solve | solution.py:36
  449.5 3.7 fusion.1
  454.4 3.6 convolution_subtract_fusion
  458.0 2.0 fusion.11
  460.0 2.4 pad_maximum_fusion
  462.4 5.6 %copy.15 = f32[4096,256]{1,0:T(8,128)} copy(f32[4096,256]{0,1:T(8,128)} %pad_maximum_fusion) | data formatting | bytes 8388608
  (41 shorter events, 5.5 us)
Async XLA Ops:
  7.2 68.7 %copy-start = (bf16[4096,256]{1,0:T(8,128)(2,1)S(1)}, bf16[4096,256]{1,0:T(8,128)(2,1)}, u32[]{:S(2)}) copy-start(bf16[4096,256]{1,0:T(8,128)(2,1)} %param.6) | copy-start | bytes 6291460
  7.2 53.8 %all-gather.4.cloned.1.call-start = ((), (), s32[]{:S(2)}) async-start(), calls=%async_computation | async-start | bytes 5242880 | tf_op jit(solution)/shard_map/all_gather | solution.py:12
  7.9 261.3 %all-reduce.3.cloned.1.call-start = ((), (), s32[]{:S(2)}) async-start(), calls=%async_computation.1 | async-start | bytes 4194304 | tf_op jit(solution)/shard_map/psum | solution.py:41
  75.8 23.4 %copy-start.5 = (bf16[2048,256]{1,0:T(8,128)(2,1)S(1)}, bf16[2048,256]{1,0:T(8,128)(2,1)}, u32[]{:S(2)}) copy-start(bf16[2048,256]{1,0:T(8,128)(2,1)} %param.8) | copy-start | bytes 3145732
  99.3 11.9 %copy-start.4 = (bf16[32,128,2048]{2,1,0:T(8,128)(2,1)S(1)}, bf16[32,128,2048]{2,1,0:T(8,128)(2,1)}, u32[]{:S(2)}) copy-start(bf16[32,128,2048]{2,1,0:T(8,128)(2,1)} %fusion) | copy-start | bytes 50331652
  109.2 2.0 copy-start.2
  117.6 259.9 %all-gather.6.cloned.1.call-start = ((), (), s32[]{:S(2)}) async-start(), calls=%async_computation.2 | async-start | bytes 33816576 | tf_op jit(solution)/shard_map/all_gather | solution.py:34
  449.5 4.9 %copy-start.3 = (f32[4096,256]{1,0:T(8,128)S(1)}, f32[4096,256]{1,0:T(8,128)}, u32[]{:S(2)}) copy-start(f32[4096,256]{1,0:T(8,128)} %copy-done.2) | copy-start | bytes 12582916
  460.0 8.0 %copy-start.1 = (bf16[4096,256]{1,0:T(8,128)(2,1)S(1)}, bf16[4096,256]{1,0:T(8,128)(2,1)}, u32[]{:S(2)}) copy-start(bf16[4096,256]{1,0:T(8,128)(2,1)} %param.6) | copy-start | bytes 6291460
Sparse Core Ops, SparseCore 0:
  9.7 51.2 all-gather.3
  117.7 151.4 all-reduce.2
  272.4 105.0 all-gather.5
